TPU v7x, 512 devices: a whole 4x8x8 slice. The times are simulated.
512 devices in a mesh: occ: 128 (over y, z, core), virt: 4 (over x).
Axes of the slice: x: 4, y: 8, z: 8, core: 2. Of those that a mesh axis runs over, the one named last changes fastest.
Arguments:
- factors: bfloat16 [768, 98304], P('virt', 'occ'), may hold values from -1 to 1
- occ_energy: float32 [64], replicated, may hold values from -2 to -0.5
- virt_energy: float32 [768], replicated, may hold values from 0.2 to 3
- pair_table: int32 [256, 2], P('occ'), may hold values from 0 to 63, as said below
- pair_count: int32 [128], P('occ'), may hold values from 0 to 2, as said below
Outputs:
- gamma: float32 [768, 98304], P('virt', 'occ')
Inputs may be any that keep to these rules, and one draw needn't show every extreme that they name: `pair_table`: each row holds two different orbitals. `pair_count`: the counts sum to exactly 128, and some host has exactly 2.
All inputs are finite; a program needn't handle non-finite values.
Results may differ from a plain program's by a relative error of at most 0.0029.
Values may be sent and summed in bfloat16 or wider, within the bound.
A program may use at most 64 MiB of HBM per device.

v0:
```python
import jax
import jax.numpy as jnp
from jax import lax
from jax.sharding import PartitionSpec as P


def laid_out(blocks, dim):
    dims = list(blocks.shape[1:])
    dims[dim] *= blocks.shape[0]
    return jnp.moveaxis(blocks, 0, dim).reshape(dims)


def gather_together(arrays, axis, dims):
    ravelled = jnp.concatenate([a.reshape(-1) for a in arrays])
    lines, at, finished = (lax.all_gather(ravelled, axis), 0, [])
    for a, dim in zip(arrays, dims):
        blocks = lines[:, at : at + a.size].reshape(-1, *a.shape)
        finished.append(laid_out(blocks, dim))
        at += a.size
    return tuple(finished)


def body(factors, occ_energy, virt_energy, pair_table, pair_count):
    tables, counts = gather_together((pair_table, pair_count), "occ", (0, 0))
    hosts_total = lax.axis_size("occ")
    per_host = pair_table.shape[0]
    entries = jnp.arange(hosts_total * per_host, dtype=jnp.int32)
    active = entries % per_host < jnp.repeat(counts, per_host)
    live_total = per_host * hosts_total // 2
    slot_count = -(-live_total // hosts_total)
    ranking = jnp.cumsum(active.astype(jnp.int32)) - 1
    targets = jnp.arange(hosts_total * slot_count, dtype=jnp.int32)
    select = (active[None, :] & (ranking[None, :] == targets[:, None])).astype(jnp.int32)
    plan = jnp.sum(select[:, :, None] * tables[None, :, :], axis=1).reshape(
        hosts_total, slot_count, 2
    )
    enabled = jnp.max(select, axis=1).reshape(hosts_total, slot_count)
    column = lax.axis_index("virt")
    myself = lax.axis_index("occ")
    orbital_count = occ_energy.shape[0]
    slab_width = factors.shape[0]
    aux_local = factors.shape[1] // orbital_count
    slab_energy = lax.dynamic_slice_in_dim(virt_energy, column * slab_width, slab_width)
    source_cube = factors.reshape(factors.shape[0], aux_local, orbital_count)

    def one_slot(position, accumulated):
        orbitals = lax.dynamic_index_in_dim(plan, position, 1, keepdims=False)
        flags = lax.dynamic_index_in_dim(enabled, position, 1, keepdims=False)
        targets_flat = orbitals.T.reshape(-1)
        picked = jnp.take(source_cube, targets_flat, axis=2)
        outgoing = picked.reshape(factors.shape[0], aux_local, 2, hosts_total)
        incoming = lax.all_to_all(outgoing, "occ", split_axis=3, concat_axis=1, tiled=True)
        both = lax.all_gather(incoming, "virt", axis=0, tiled=True)
        left = both[:, :, 0, 0]
        right = both[:, :, 1, 0]
        mine = lax.dynamic_index_in_dim(orbitals, myself, 0, keepdims=False)
        live_here = lax.dynamic_index_in_dim(flags, myself, 0, keepdims=False).astype(jnp.float32)
        left_slab = lax.dynamic_slice_in_dim(left, column * slab_width, slab_width, 0)
        right_slab = lax.dynamic_slice_in_dim(right, column * slab_width, slab_width, 0)
        couple_rows = lax.dot_general(
            left_slab, right, (((1,), (1,)), ((), ())), preferred_element_type=jnp.float32
        )
        couple_cols = lax.dot_general(
            left, right_slab, (((1,), (1,)), ((), ())), preferred_element_type=jnp.float32
        )
        energy_sum = jnp.take(occ_energy, mine[0]) + jnp.take(occ_energy, mine[1])
        ampl_rows = couple_rows / (energy_sum - slab_energy[:, None] - virt_energy[None, :])
        ampl_cols = couple_cols / (energy_sum - virt_energy[:, None] - slab_energy[None, :])
        mixed_rows = ((2.0 * ampl_rows - ampl_cols.T) * live_here).astype(jnp.bfloat16)
        mixed_cols = ((2.0 * ampl_cols - ampl_rows.T) * live_here).astype(jnp.bfloat16)
        toward_first = jnp.dot(mixed_rows, right, preferred_element_type=jnp.float32)
        toward_second = lax.dot_general(
            mixed_cols, left, (((0,), (0,)), ((), ())), preferred_element_type=jnp.float32
        )
        packed = jnp.stack(
            [toward_first.astype(jnp.bfloat16), toward_second.astype(jnp.bfloat16)], axis=2
        )
        packed = packed.reshape(slab_width, hosts_total, aux_local, 2, 1)
        returned = lax.all_to_all(packed, "occ", split_axis=1, concat_axis=4, tiled=True)
        onehot = (
            targets_flat[:, None] == jnp.arange(orbital_count, dtype=jnp.int32)[None, :]
        ).astype(jnp.bfloat16)
        added = jnp.dot(
            returned.reshape(slab_width * aux_local, 2 * hosts_total),
            onehot,
            preferred_element_type=jnp.float32,
        )
        return accumulated + added.reshape(accumulated.shape)

    start = jnp.zeros(factors.shape, jnp.float32)
    return lax.fori_loop(0, slot_count, one_slot, start)


def solution(mesh):
    in_specs = (P("virt", "occ"), P(), P(), P("occ", None), P("occ"))
    out_specs = P("virt", "occ")
    return jax.shard_map(body, mesh=mesh, in_specs=in_specs, out_specs=out_specs, check_vma=False)
```

profile of v0, /device:TPU:8, one launch (start us, length us, event | category | flops | bytes accessed | tf_op | source)
XLA Modules:
  0.0 244.5 jit_solution(16003386581368237176)
XLA Ops:
  6.5 1.1 copy.56
  8.5 0.8 reshape.178
  9.3 1.3 dynamic-slice.11
  11.4 31.4 %all-reduce = s32[640]{0:T(1024)S(1)} all-reduce(s32[640]{0:T(1024)S(1)} %add_dynamic-update-slice_fusion), channel_id=2, replica_groups=mesh['occ'=128,'virt'=4] {'occ'}, use_global_device_ids=true, to_apply=%add | all-reduce | flops 640 | bytes 5120
  44.8 0.8 gather_fusion
  45.5 2.8 %copy.69 = bf16[192,12,2,128]{3,2,0,1:T(2,128)(2,1)} copy(bf16[192,12,2,128]{0,1,3,2:T(8,128)(2,1)S(1)} %bitcast.73) | data formatting | bytes 2359296 | tf_op jit(solution)/shard_map/while/body/eval_jaxpr/jit(_take)/gather | solution.py:50
  48.3 2.3 broadcast_select_fusion
  50.6 3.2 %copy.59 = bf16[192,12,2,128]{0,2,1,3:T(2,128)(2,1)S(1)} copy(bf16[192,12,2,128]{3,2,0,1:T(2,128)(2,1)S(1)} %broadcast_select_fusion) | data formatting | bytes 2359296 | tf_op jit(solution)/shard_map/while/body/eval_jaxpr/jit(_take)/select_n | solution.py:50
  53.8 48.7 %all_to_all.41 = bf16[192,12,2,128]{0,2,1,3:T(2,128)(2,1)S(1)} all-to-all(bf16[192,12,2,128]{0,2,1,3:T(2,128)(2,1)S(1)} %copy.59), channel_id=1, replica_groups=mesh['occ'=128,'virt'=4] {'occ'}, dimensions={3} | all-to-all | bytes 2359296 | tf_op jit(solution)/shard_map/while/body/eval_jaxpr/all_to_all | solution.py:52
  102.5 4.4 %copy.60 = bf16[192,1536,2,1]{1,2,3,0:T(2,128)(2,1)} copy(bf16[192,1536,2,1]{0,2,1,3:T(2,128)(2,1)S(1)} %bitcast.74) | data formatting | bytes 2359296 | tf_op jit(solution)/shard_map/while/body/eval_jaxpr/all_to_all | solution.py:52
  107.0 0.6 fusion.44
  111.7 0.6 dynamic_slice.37
  113.0 0.6 fusion.45
  114.9 43.6 %all-gather.3.cloned.1.call-done = bf16[768,1536,2,1]{1,2,3,0:T(2,128)(2,1)} async-done(((bf16[192,1536,2,1]{1,2,3,0:T(2,128)(2,1)}), bf16[768,1536,2,1]{1,2,3,0:T(2,128)(2,1)}) %all-gather.3.cloned.1.call-update) | async-done | bytes 4718608 | tf_op jit(solution)/shard_map/while/body/eval_jaxpr/all_gather | solution.py:53
  158.5 9.6 %fusion.43 = (bf16[768,1536,1,1]{1,2,3,0:T(2,128)(2,1)S(1)}, bf16[768,1536,1,1]{1,2,3,0:T(2,128)(2,1)S(1)}) fusion(bf16[768,1536,2,1]{1,2,3,0:T(2,128)(2,1)} %all-gather.3.cloned.1.call-done), kind=kLoop, calls=%fused_computation.67 | loop fusion | bytes 9437184 | tf_op jit(solution)/shard_map/while/body/eval_jaxpr/slice | solution.py:55
  168.2 0.6 copy.70
  169.4 0.9 fusion.4
  170.3 0.9 fusion.1
  171.2 0.8 convolution_convert_fusion
  172.0 0.8 convolution_convert_fusion.1
  174.3 2.4 copy.65
  176.7 56.3 %all_to_all.42 = bf16[192,128,12,2,1]{0,3,4,2,1:T(2,128)(2,1)S(1)} all-to-all(bf16[192,128,12,2,1]{0,3,4,2,1:T(2,128)(2,1)S(1)} %copy.65), channel_id=1, replica_groups=mesh['occ'=128,'virt'=4] {'occ'}, dimensions={1} | all-to-all | bytes 2359296 | tf_op jit(solution)/shard_map/while/body/eval_jaxpr/all_to_all | solution.py:79
  233.0 2.9 %copy.66 = bf16[192,1,12,2,128,1]{4,3,2,0,5,1:T(2,128)(2,1)S(1)} copy(bf16[192,1,12,2,128,1]{0,3,2,4,5,1:T(2,128)(2,1)S(1)} %bitcast.75) | data formatting | bytes 2359296 | tf_op jit(solution)/shard_map/while/body/eval_jaxpr/all_to_all | solution.py:79
  236.5 1.1 reshape.186
  (41 shorter events, 5.1 us)
Async XLA Ops:
  6.5 152.0 %all-gather.3.cloned.1.call-start = ((), (), s32[]{:S(2)}) async-start(), calls=%async_computation.2 | async-start | bytes 5898240 | tf_op jit(solution)/shard_map/while/body/eval_jaxpr/all_gather | solution.py:53
  102.5 10.5 %copy-start.1 = (f32[64]{0:T(128)S(1)}, f32[64]{0:T(128)}, u32[]{:S(2)}) copy-start(f32[64]{0:T(128)} %param.6) | copy-start | bytes 772
  102.5 12.3 %copy-start = (f32[768]{0:T(1024)S(1)}, f32[768]{0:T(1024)}, u32[]{:S(2)}) copy-start(f32[768]{0:T(1024)} %param.7) | copy-start | bytes 9220
Sparse Core Ops, SparseCore 0:
  107.0 51.4 all-gather.2
where the time goes:
time: 245 us; the launch traced here: 244 us
  blocking collectives  136 us (56%)
  waiting for transfers between devices  43.6 us (18%)
  local copies, waits for them, and re-layouts  36 us (15%)
  between operations  20.8 us (8%)
  matrix products  3.96 us (2%)
  other arithmetic  3.7 us (2%)
    all_to_all x1, blocking collectives, one_slot(): lax.all_to_all(packed, 'occ', split_axis=1, concat_axis=4, tiled=True)  56.3 us
    all_to_all x1, blocking collectives, one_slot(): lax.all_to_all(outgoing, 'occ', split_axis=3, concat_axis=1, tiled=True)  48.7 us
    all_gather x1, waiting for transfers between devices, one_slot(): both = lax.all_gather(incoming, 'virt', axis=0, tiled=True)  43.6 us
    unnamed x1, blocking collectives  31.4 us
    slice x1, local copies, waits for them, and re-layouts, one_slot(): right = both[:, :, 1, 0]  9.63 us
  transfers between devices with their start and end apart: 1, of which 1 were waited for; matrix products, arithmetic and copies ran while one was open for 1% of the time, Pallas kernels for 0%

commit v1 on v0

--- a/solution.py
+++ b/solution.py
@@ -2,6 +2,28 @@
 import jax.numpy as jnp
 from jax import lax
 from jax.sharding import PartitionSpec as P
+
+
+def joined_along(tiles, dim):
+    tiles = jnp.moveaxis(tiles, 0, dim)
+    dims = tiles.shape
+    return tiles.reshape(*dims[:dim], dims[dim] * dims[dim + 1], *dims[dim + 2 :])
+
+
+def collect(x, axis, dim):
+    count = lax.axis_size(axis)
+    pairs = [(i, (i + 1) % count) for i in range(count)]
+    back = [(b, a) for a, b in pairs]
+    lower, upper = ([], [])
+    for step in range(count - 1):
+        if step % 2 == 0:
+            lower.append(lax.ppermute(lower[-1] if lower else x, axis, pairs))
+        else:
+            upper.append(lax.ppermute(upper[-1] if upper else x, axis, back))
+    tiles = jnp.stack([*lower[::-1], x, *upper])
+    shift = lax.axis_index(axis) - len(lower)
+    tiles = tiles[(jnp.arange(count) - shift) % count]
+    return joined_along(tiles, dim)
 
 
 def laid_out(blocks, dim):
@@ -50,7 +72,7 @@
         picked = jnp.take(source_cube, targets_flat, axis=2)
         outgoing = picked.reshape(factors.shape[0], aux_local, 2, hosts_total)
         incoming = lax.all_to_all(outgoing, "occ", split_axis=3, concat_axis=1, tiled=True)
-        both = lax.all_gather(incoming, "virt", axis=0, tiled=True)
+        both = collect(incoming, "virt", 0)
         left = both[:, :, 0, 0]
         right = both[:, :, 1, 0]
         mine = lax.dynamic_index_in_dim(orbitals, myself, 0, keepdims=False)

time: 245 us -> 231 us (0.943)
  between operations: 20.8 us -> 7.22 us
  starting transfers between devices: 0.01 us -> 9.4 us
  waiting for transfers between devices: 43.6 us -> 35.1 us
  other arithmetic: 3.7 us -> 7.47 us
  local copies, waits for them, and re-layouts: 36 us -> 33.5 us
    all_gather x1 -> x0, waiting for transfers between devices: 43.6 us -> none  [one_slot(): both = lax.all_gather(incoming, 'virt', axis=0, tiled=True)]
    ppermute x0 -> x3, waiting for transfers between devices: none -> 35.1 us  [the longest x2 35.1 us: collect(): lower.append(lax.ppermute(lower[-1] if lower else x, axis, pairs))]
    ppermute x0 -> x3, starting transfers between devices: none -> 9.4 us  [the longest x2 5.76 us: collect(): lower.append(lax.ppermute(lower[-1] if lower else x, axis, pairs))]
    slice x1, local copies, waits for them, and re-layouts: 9.63 us -> 0.31 us  [one_slot(): right = both[:, :, 1, 0]]
    gather x0 -> x2, local copies, waits for them, and re-layouts: none -> 7.99 us  [collect(): tiles = tiles[(jnp.arange(count) - shift) % count]]
    another operation x2 -> x3, other arithmetic: 0.35 us -> 4.18 us  [the longest x1 3.83 us: collect(): tiles = jnp.stack([*lower[::-1], x, *upper])]
    all_to_all x1, blocking collectives: 56.3 us -> 53.5 us  [one_slot(): lax.all_to_all(packed, 'occ', split_axis=1, concat_axis=4, tiled=True)]
  transfers between devices with their start and end apart: 1 -> 3, of which waited for: 1 -> 2; matrix products, arithmetic and copies ran while one was open for 1% -> 3% of each run, Pallas kernels for 0% -> 0%
where the time goes in v1:
time: 231 us; the launch traced here: 230 us
  blocking collectives  134 us (58%)
  waiting for transfers between devices  35.1 us (15%)
  local copies, waits for them, and re-layouts  33.5 us (15%)
  starting transfers between devices  9.4 us (4%)
  other arithmetic  7.47 us (3%)
  between operations  7.22 us (3%)
  matrix products  3.98 us (2%)
    all_to_all x1, blocking collectives, one_slot(): lax.all_to_all(packed, 'occ', split_axis=1, concat_axis=4, tiled=True)  53.5 us
    all_to_all x1, blocking collectives, one_slot(): lax.all_to_all(outgoing, 'occ', split_axis=3, concat_axis=1, tiled=True)  48.7 us
    ppermute x2, waiting for transfers between devices, collect(): lower.append(lax.ppermute(lower[-1] if lower else x, axis, pairs))  35.1 us
    unnamed x1, blocking collectives  31.4 us
    gather x2, local copies, waits for them, and re-layouts, collect(): tiles = tiles[(jnp.arange(count) - shift) % count]  7.99 us
    ppermute x2, starting transfers between devices, collect(): lower.append(lax.ppermute(lower[-1] if lower else x, axis, pairs))  5.76 us
  transfers between devices with their start and end apart: 3, of which 2 were waited for; matrix products, arithmetic and copies ran while one was open for 3% of the time, Pallas kernels for 0%

profile of v1, /device:TPU:8, one launch (start us, length us, event | category | flops | bytes accessed | tf_op | source)
XLA Modules:
  0.0 230.3 jit_solution(18121859408664538437)
XLA Ops:
  1.4 1.3 dynamic-slice.11
  3.5 31.4 %all-reduce = s32[640]{0:T(1024)S(1)} all-reduce(s32[640]{0:T(1024)S(1)} %add_dynamic-update-slice_fusion), channel_id=2, replica_groups=mesh['occ'=128,'virt'=4] {'occ'}, use_global_device_ids=true, to_apply=%add | all-reduce | flops 640 | bytes 5120
  36.9 1.1 copy.69
  39.0 2.1 copy.85
  41.1 1.0 broadcast_select_fusion
  42.1 3.2 %copy.72 = bf16[192,12,2,128]{0,2,1,3:T(2,128)(2,1)S(1)} copy(bf16[192,12,2,128]{3,2,0,1:T(2,128)(2,1)S(1)} %broadcast_select_fusion) | data formatting | bytes 2359296 | tf_op jit(solution)/shard_map/while/body/eval_jaxpr/jit(_take)/select_n | solution.py:72
  45.3 48.7 %all_to_all.41 = bf16[192,12,2,128]{0,2,1,3:T(2,128)(2,1)S(1)} all-to-all(bf16[192,12,2,128]{0,2,1,3:T(2,128)(2,1)S(1)} %copy.72), channel_id=1, replica_groups=mesh['occ'=128,'virt'=4] {'occ'}, dimensions={3} | all-to-all | bytes 2359296 | tf_op jit(solution)/shard_map/while/body/eval_jaxpr/all_to_all | solution.py:74
  94.0 1.1 copy.73
  95.1 3.4 %collective-permute-start = (bf16[192,1536,2,1]{1,0,2,3:T(8,128)(2,1)S(1)}, bf16[192,1536,2,1]{1,0,2,3:T(8,128)(2,1)}, u32[]{:S(2)}, u32[]{:S(2)}) collective-permute-start(bf16[192,1536,2,1]{1,0,2,3:T(8,128)(2,1)S(1)} %copy.73), channel_id=1, source_target_pairs={{0,1},{1,2},{2,3},{3,0},{4,5},{5,6},{6,7},{7,4},{8,9},{9,10},{10,1... | collective-permute-start | bytes 3538952 | tf_op jit(solution)/shard_map/while/body/eval_jaxpr/ppermute | solution.py:20
  98.5 2.9 %copy.74 = bf16[192,1536,2,1]{1,0,3,2:T(8,128)(2,1)} copy(bf16[192,1536,2,1]{0,2,1,3:T(2,128)(2,1)S(1)} %bitcast.88) | data formatting | bytes 2359296 | tf_op jit(solution)/shard_map/while/body/eval_jaxpr/all_to_all | solution.py:74
  101.5 3.6 %collective-permute-start.2 = (bf16[192,1536,2,1]{1,0,3,2:T(8,128)(2,1)}, bf16[192,1536,2,1]{1,0,3,2:T(8,128)(2,1)}, u32[]{:S(2)}, u32[]{:S(2)}) collective-permute-start(bf16[192,1536,2,1]{1,0,3,2:T(8,128)(2,1)} %copy.74), channel_id=1, source_target_pairs={{1,0},{2,1},{3,2},{0,3},{5,4},{6,5},{7,6},{4,7},{9,8},{10,9},{11,1... | collective-permute-start | bytes 3538952 | tf_op jit(solution)/shard_map/while/body/eval_jaxpr/ppermute | solution.py:22
  105.1 19.0 %collective-permute-done = bf16[192,1536,2,1]{1,0,2,3:T(8,128)(2,1)} collective-permute-done((bf16[192,1536,2,1]{1,0,2,3:T(8,128)(2,1)S(1)}, bf16[192,1536,2,1]{1,0,2,3:T(8,128)(2,1)}, u32[]{:S(2)}, u32[]{:S(2)}) %collective-permute-start) | collective-permute-done | bytes 1179680 | tf_op jit(solution)/shard_map/while/body/eval_jaxpr/ppermute | solution.py:20
  124.1 2.4 %collective-permute-start.1 = (bf16[192,1536,2,1]{1,0,2,3:T(8,128)(2,1)}, bf16[192,1536,2,1]{1,0,2,3:T(8,128)(2,1)}, u32[]{:S(2)}, u32[]{:S(2)}) collective-permute-start(bf16[192,1536,2,1]{1,0,2,3:T(8,128)(2,1)} %collective-permute-done), channel_id=1, source_target_pairs={{0,1},{1,2},{2,3},{3,0},{4,5},{5,6},{6,7},{7,4},{8,9},{9,10},{10,1... | collective-permute-start | bytes 3538952 | tf_op jit(solution)/shard_map/while/body/eval_jaxpr/ppermute | solution.py:20
  135.3 1.1 copy.76
  136.5 16.0 %collective-permute-done.1 = bf16[192,1536,2,1]{1,0,2,3:T(8,128)(2,1)} collective-permute-done((bf16[192,1536,2,1]{1,0,2,3:T(8,128)(2,1)}, bf16[192,1536,2,1]{1,0,2,3:T(8,128)(2,1)}, u32[]{:S(2)}, u32[]{:S(2)}) %collective-permute-start.1) | collective-permute-done | bytes 1179680 | tf_op jit(solution)/shard_map/while/body/eval_jaxpr/ppermute | solution.py:20
  152.5 3.8 %maximum_bitcast_fusion = bf16[4,192,1536,2]{2,1,3,0:T(8,128)(2,1)} fusion(bf16[1,192,1536,2,1]{2,1,3,0,4:T(8,128)(2,1)} %bitcast.19, bf16[1,192,1536,2,1]{2,1,3,0,4:T(8,128)(2,1)S(1)} %copy.76, bf16[1,192,1536,2,1]{2,1,3,0,4:T(8,128)(2,1)} %bitcast.14, bf16[1,192,1536,2,1]{2,1,3,0,4:T(8,128)(2,1)} %bitcast.13), kind=kLoop, calls=%fused_computation.2 | loop fusion | flops 7077888 | bytes 9437184 | tf_op jit(solution)/shard_map/while/body/eval_jaxpr/stack | solution.py:23
  156.3 5.4 %gather_fusion.1 = bf16[4,192,1536,2]{2,1,3,0:T(8,128)(2,1)} fusion(bf16[4,192,1536,2]{2,1,3,0:T(8,128)(2,1)} %maximum_bitcast_fusion, s32[1024]{0:T(1024)S(1)} %pad_clamp_fusion), kind=kCustom, calls=%fused_computation.1 | custom fusion | bytes 9437200 | tf_op jit(solution)/shard_map/while/body/eval_jaxpr/gather | solution.py:25
  161.7 2.6 %copy.78 = bf16[4,192,1536,2]{2,1,0,3:T(8,128)(2,1)S(1)} copy(bf16[4,192,1536,2]{2,1,3,0:T(8,128)(2,1)} %gather_fusion.1) | data formatting | bytes 9437184 | tf_op jit(solution)/shard_map/while/body/eval_jaxpr/gather | solution.py:25
  164.6 0.9 fusion.1
  165.6 0.9 fusion.4
  169.7 2.4 %copy.81 = bf16[192,128,12,2,1]{0,3,4,2,1:T(2,128)(2,1)S(1)} copy(bf16[192,128,12,2,1]{0,2,1,4,3:T(8,128)(2,1)S(1)} %pad_maximum_fusion) | data formatting | bytes 2359296 | tf_op jit(solution)/shard_map/while/body/eval_jaxpr/stack | solution.py:97
  172.1 53.5 %all_to_all.42 = bf16[192,128,12,2,1]{0,3,4,2,1:T(2,128)(2,1)S(1)} all-to-all(bf16[192,128,12,2,1]{0,3,4,2,1:T(2,128)(2,1)S(1)} %copy.81), channel_id=1, replica_groups=mesh['occ'=128,'virt'=4] {'occ'}, dimensions={1} | all-to-all | bytes 2359296 | tf_op jit(solution)/shard_map/while/body/eval_jaxpr/all_to_all | solution.py:101
  225.7 2.9 %copy.82 = bf16[192,1,12,2,128,1]{4,3,2,0,5,1:T(2,128)(2,1)S(1)} copy(bf16[192,1,12,2,128,1]{0,3,2,4,5,1:T(2,128)(2,1)S(1)} %bitcast.96) | data formatting | bytes 2359296 | tf_op jit(solution)/shard_map/while/body/eval_jaxpr/all_to_all | solution.py:101
  229.1 1.1 reshape.241
  (61 shorter events, 11.0 us)
Async XLA Ops:
  36.8 89.7 %copy-start = (s32[128,2]{0,1:T(2,128)}, s32[128,2]{0,1:T(2,128)S(1)}, u32[]{:S(2)}) copy-start(s32[128,2]{0,1:T(2,128)S(1)} %multiply_reduce_fusion) | copy-start | bytes 3076
  94.0 38.1 %copy-start.5 = (f32[64]{0:T(128)S(1)}, f32[64]{0:T(128)}, u32[]{:S(2)}) copy-start(f32[64]{0:T(128)} %param.6) | copy-start | bytes 772
  94.0 40.0 %copy-start.2 = (f32[768]{0:T(1024)S(1)}, f32[768]{0:T(1024)}, u32[]{:S(2)}) copy-start(f32[768]{0:T(1024)} %param.7) | copy-start | bytes 9220
  95.1 29.0 %collective-permute-start = (bf16[192,1536,2,1]{1,0,2,3:T(8,128)(2,1)S(1)}, bf16[192,1536,2,1]{1,0,2,3:T(8,128)(2,1)}, u32[]{:S(2)}, u32[]{:S(2)}) collective-permute-start(bf16[192,1536,2,1]{1,0,2,3:T(8,128)(2,1)S(1)} %copy.73), channel_id=1, source_target_pairs={{0,1},{1,2},{2,3},{3,0},{4,5},{5,6},{6,7},{7,4},{8,9},{9,10},{10,1... | collective-permute-start | bytes 3538952 | tf_op jit(solution)/shard_map/while/body/eval_jaxpr/ppermute | solution.py:20
  101.5 35.0 %collective-permute-start.2 = (bf16[192,1536,2,1]{1,0,3,2:T(8,128)(2,1)}, bf16[192,1536,2,1]{1,0,3,2:T(8,128)(2,1)}, u32[]{:S(2)}, u32[]{:S(2)}) collective-permute-start(bf16[192,1536,2,1]{1,0,3,2:T(8,128)(2,1)} %copy.74), channel_id=1, source_target_pairs={{1,0},{2,1},{3,2},{0,3},{5,4},{6,5},{7,6},{4,7},{9,8},{10,9},{11,1... | collective-permute-start | bytes 3538952 | tf_op jit(solution)/shard_map/while/body/eval_jaxpr/ppermute | solution.py:22
  124.1 28.3 %collective-permute-start.1 = (bf16[192,1536,2,1]{1,0,2,3:T(8,128)(2,1)}, bf16[192,1536,2,1]{1,0,2,3:T(8,128)(2,1)}, u32[]{:S(2)}, u32[]{:S(2)}) collective-permute-start(bf16[192,1536,2,1]{1,0,2,3:T(8,128)(2,1)} %collective-permute-done), channel_id=1, source_target_pairs={{0,1},{1,2},{2,3},{3,0},{4,5},{5,6},{6,7},{7,4},{8,9},{9,10},{10,1... | collective-permute-start | bytes 3538952 | tf_op jit(solution)/shard_map/while/body/eval_jaxpr/ppermute | solution.py:20
  165.5 1.0 copy-start.3
  165.6 1.0 copy-start.4
  165.6 1.0 copy-start.6
  165.6 1.0 copy-start.7
  172.1 56.5 %copy-start.1 = (s32[128,2]{0,1:T(2,128)S(1)}, s32[128,2]{0,1:T(2,128)}, u32[]{:S(2)}) copy-start(s32[128,2]{0,1:T(2,128)} %copy-done) | copy-start | bytes 3076
